TPU v7x, 32 devices: a whole 2x2x4 slice. The times are simulated.
32 devices in a mesh: dp: 8 (over z, y), mp: 4 (over x, core).
Axes of the slice: x: 2, y: 2, z: 4, core: 2. Of those that a mesh axis runs over, the one named last changes fastest.
Arguments:
- hidden_in: bfloat16 [32768, 768], P(('dp', 'mp')), may hold values from -37 to 37
- out_grad: bfloat16 [32768, 768], P(('dp', 'mp')), may hold values from -18 to 18
- seq_len: int32 [8], P('dp'), may hold values from 1024 to 4096, as said below
- owner_list: int32 [24], replicated, may hold values from 0 to 7, as said below
- block_master: float32 [4, 8, 768, 194], P('mp', 'dp'), may hold values from -0.4690971 to 0.4690971
- block_first: float32 [4, 8, 768, 194], P('mp', 'dp'), may hold values from -2048 to 2048
- block_second: float32 [4, 8, 768, 194], P('mp', 'dp'), may hold values from 131072 to 524288
- block_ema: float32 [4, 8, 768, 194], P('mp', 'dp'), may hold values from -0.21875 to 0.21875
- head_small: float32 [24, 10, 64], P('mp'), may hold values from -10 to 3
- head_first: float32 [24, 10, 64], P('mp'), may hold values from -1024 to 1024
- head_second: float32 [24, 10, 64], P('mp'), may hold values from 32768 to 131072
- head_ema: float32 [24, 10, 64], P('mp'), may hold values from -6 to 6
- bc_weight: float32 [768, 256], replicated, may hold values from -0.21875 to 0.21875
- bc_first: float32 [768, 256], replicated, may hold values from -1024 to 1024
- bc_second: float32 [768, 256], replicated, may hold values from 32768 to 131072
- bc_ema: float32 [768, 256], replicated, may hold values from -0.21875 to 0.21875
- shared_small: float32 [10, 256], replicated, may hold values from 0.25 to 1.25
- shared_first: float32 [10, 256], replicated, may hold values from -1024 to 1024
- shared_second: float32 [10, 256], replicated, may hold values from 32768 to 131072
- shared_ema: float32 [10, 256], replicated, may hold values from 0.25 to 1.25
Outputs:
- hidden_out: bfloat16 [32768, 768], P(('dp', 'mp'))
- hidden_grad: float32 [32768, 768], P(('dp', 'mp'))
- block_master_new: float32 [4, 8, 768, 194], P('mp', 'dp')
- block_first_new: float32 [4, 8, 768, 194], P('mp', 'dp')
- block_second_new: float32 [4, 8, 768, 194], P('mp', 'dp')
- block_ema_new: float32 [4, 8, 768, 194], P('mp', 'dp')
- head_small_new: float32 [24, 10, 64], P('mp')
- head_first_new: float32 [24, 10, 64], P('mp')
- head_second_new: float32 [24, 10, 64], P('mp')
- head_ema_new: float32 [24, 10, 64], P('mp')
- bc_weight_new: float32 [768, 256], replicated
- bc_first_new: float32 [768, 256], replicated
- bc_second_new: float32 [768, 256], replicated
- bc_ema_new: float32 [768, 256], replicated
- shared_small_new: float32 [10, 256], replicated
- shared_first_new: float32 [10, 256], replicated
- shared_second_new: float32 [10, 256], replicated
- shared_ema_new: float32 [10, 256], replicated
Inputs may be any that keep to these rules, and one draw needn't show every extreme that they name: `seq_len`: all sequences of a group have the same length, one of 1024, 2048, 4096; each of the three occurs in every draw. `owner_list`: the 6 heads of one index of mp (heads i * 6 to (i + 1) * 6 - 1) have distinct owners.
All inputs are finite; a program needn't handle non-finite values.
Results may differ from a plain program's by a relative error of at most 0.01.
Values may be sent and summed in bfloat16 or wider, within the bound.
No kernel may reach another device: no remote copies, remote signals or barrier semaphores. Data moves between devices by JAX's collectives and lax.ppermute only.
A program may use at most 448 MiB of HBM per device.

v0:
```python
import jax
import jax.numpy as jnp
from jax import lax
from jax.sharding import PartitionSpec as P

D = 768
H = 24
P_SIZE = 64
K = 7
BLOCK_LEN = 256
STEP = 3
PRECISE = lax.Precision.HIGHEST
NORM_EPS = 1e-05
BETA_ONE = 0.5
BETA_TWO = 0.5
ADAM_EPS = 1e-08
WEIGHT_DECAY = 0.1
MATRIX_RATE = 0.04
SMALL_RATE = 0.2
AVERAGE_KEEP = 0.75


def conv_centered(signal, filter_taps, seq_length):
    row_count = signal.shape[0]
    tap_count = filter_taps.shape[0]
    half_taps = tap_count // 2
    position = jnp.arange(row_count, dtype=jnp.int32) % seq_length
    padded = jnp.pad(signal, ((half_taps, half_taps), (0, 0)))
    summed = jnp.zeros_like(signal)
    for tap_index in range(tap_count):
        offset = tap_index - half_taps
        shifted = padded[tap_index : tap_index + row_count]
        inside = (position + offset >= 0) & (position + offset < seq_length)
        summed = summed + jnp.where(inside[:, None], shifted, 0.0) * filter_taps[tap_index][None, :]
    return summed


def shift_down(values, seq_length):
    shifted = jnp.concatenate([jnp.zeros_like(values[:1]), values[:-1]], axis=0)
    position = jnp.arange(values.shape[0], dtype=jnp.int32) % seq_length
    return jnp.where((position > 0)[:, None, None], shifted, 0.0)


def within_blocks(values_blk, b_blk, c_blk, rates_blk):
    log_decay = jnp.transpose(jnp.cumsum(-rates_blk, axis=1), (0, 2, 1))
    block_size = rates_blk.shape[1]
    scores = jnp.einsum("bin,bjn->bij", c_blk, b_blk, precision=PRECISE)
    causal_mask = (jnp.arange(block_size)[:, None] >= jnp.arange(block_size)[None, :])[None, None]
    log_gap = log_decay[:, :, :, None] - log_decay[:, :, None, :]
    decay_mat = jnp.where(causal_mask, jnp.exp(jnp.where(causal_mask, log_gap, -60.0)), 0.0)
    weights = decay_mat * scores[:, None] * jnp.transpose(rates_blk, (0, 2, 1))[:, :, None, :]
    inner_part = jnp.einsum("bhij,bjhp->bihp", weights, values_blk, precision=PRECISE)
    tail_decay = jnp.exp(log_decay[:, :, -1:] - log_decay) * jnp.transpose(rates_blk, (0, 2, 1))
    local_state = jnp.einsum("bjn,bhj,bjhp->bhnp", b_blk, tail_decay, values_blk, precision=PRECISE)
    return (inner_part, local_state, log_decay)


def carry_state(state_in, pieces):
    local_state, total_decay, keep_flag = pieces
    entering = state_in * keep_flag
    new_state = entering * jnp.exp(total_decay)[:, None, None] + local_state
    return (new_state, entering)


def state_mix(values, b_vectors, c_vectors, step_rates, seq_length):
    row_count, head_count, head_width = values.shape
    blocks = row_count // BLOCK_LEN
    keep_flags = (jnp.arange(blocks, dtype=jnp.int32) * BLOCK_LEN % seq_length != 0).astype(
        jnp.float32
    )
    values_blk = values.reshape(blocks, BLOCK_LEN, head_count, head_width)
    b_blk = b_vectors.reshape(blocks, BLOCK_LEN, -1)
    c_blk = c_vectors.reshape(blocks, BLOCK_LEN, -1)
    rates_blk = step_rates.reshape(blocks, BLOCK_LEN, head_count)
    inner_part, local_state, log_decay = jax.checkpoint(within_blocks)(
        values_blk, b_blk, c_blk, rates_blk
    )
    initial = jnp.zeros((head_count, b_vectors.shape[1], head_width), jnp.float32)
    _, entering_all = lax.scan(carry_state, initial, (local_state, log_decay[:, :, -1], keep_flags))
    cross_part = jnp.einsum("bin,bhnp->bihp", c_blk, entering_all, precision=PRECISE)
    cross_part = cross_part * jnp.transpose(jnp.exp(log_decay), (0, 2, 1))[:, :, :, None]
    return (inner_part + cross_part).reshape(row_count, head_count, head_width)


def local_mix(proj_heads, proj_keys, head_params, key_taps, seq_length):
    row_count, head_count, _ = proj_heads.shape
    head_width = head_params.shape[2]
    tap_count = key_taps.shape[0]
    gate_part = proj_heads[:, :, :head_width]
    value_part = proj_heads[:, :, head_width : 2 * head_width].reshape(
        row_count, head_count * head_width
    )
    rate_part = proj_heads[:, :, 2 * head_width : 2 * head_width + 2]
    value_taps = jnp.transpose(head_params[:, 1 : 1 + tap_count, :], (1, 0, 2)).reshape(
        tap_count, head_count * head_width
    )
    values = jax.nn.silu(conv_centered(value_part, value_taps, seq_length)).reshape(
        row_count, head_count, head_width
    )
    key_signal = jax.nn.silu(conv_centered(proj_keys, key_taps, seq_length))
    state_size = key_signal.shape[1] // 4
    forward_b = key_signal[:, :state_size]
    forward_c = key_signal[:, state_size : 2 * state_size]
    reverse_b = key_signal[:, 2 * state_size : 3 * state_size]
    reverse_c = key_signal[:, 3 * state_size :]
    step_rates = jax.nn.softplus(rate_part + head_params[None, :, tap_count + 2, :2])
    diagonal = head_params[:, tap_count + 1, :]
    forward = shift_down(
        state_mix(values, forward_b, forward_c, step_rates[:, :, 0], seq_length), seq_length
    )
    backward = shift_down(
        state_mix(
            values[::-1], reverse_b[::-1], reverse_c[::-1], step_rates[::-1, :, 1], seq_length
        ),
        seq_length,
    )[::-1]
    mixture = forward + backward + values * diagonal[None]
    return mixture * jax.nn.silu(gate_part)


def adamw_update(weight, gradient, first_moment, second, average, step_rate):
    first_new = BETA_ONE * first_moment + (1.0 - BETA_ONE) * gradient
    second_new = BETA_TWO * second + (1.0 - BETA_TWO) * gradient * gradient
    correct_one = 1.0 - BETA_ONE**STEP
    correct_two = 1.0 - BETA_TWO**STEP
    normalized = first_new / correct_one / (jnp.sqrt(second_new / correct_two) + ADAM_EPS)
    weight_new = weight - step_rate * (normalized + WEIGHT_DECAY * weight)
    average_new = AVERAGE_KEEP * average + (1.0 - AVERAGE_KEEP) * weight_new
    return (weight_new, first_new, second_new, average_new)


def local(
    hidden_in,
    out_grad,
    seq_len,
    owner_list,
    block_master,
    block_first,
    block_second,
    block_ema,
    head_small,
    head_first,
    head_second,
    head_ema,
    bc_weight,
    bc_first,
    bc_second,
    bc_ema,
    shared_small,
    shared_first,
    shared_second,
    shared_ema,
):
    heads_here = head_small.shape[0]
    mp_index = lax.axis_index("mp")
    dp_index = lax.axis_index("dp")
    seq_length = seq_len[0]
    owners_here = lax.dynamic_slice_in_dim(owner_list, mp_index * heads_here, heads_here)
    slot_low = block_master[0].astype(jnp.bfloat16)
    all_slots = lax.all_gather(slot_low, "dp", axis=0, tiled=True)
    blocks = jnp.take(all_slots, owners_here, axis=0)
    in_width = 2 * P_SIZE + 2
    w_in_flat = jnp.transpose(blocks[:, :, :in_width], (1, 0, 2)).reshape(D, heads_here * in_width)
    w_out_flat = jnp.transpose(blocks[:, :, in_width:], (0, 2, 1)).reshape(heads_here * P_SIZE, D)
    key_low = bc_weight.astype(jnp.bfloat16)
    key_taps = shared_small[:K]
    gain_in = shared_small[K:].reshape(D)
    hidden = hidden_in.astype(jnp.float32)
    scale_in = lax.rsqrt(jnp.mean(hidden * hidden, axis=1, keepdims=True) + NORM_EPS)
    normed_low = (hidden * scale_in * gain_in).astype(jnp.bfloat16)
    features = lax.all_gather(normed_low, "mp", axis=0, tiled=True)
    group_rows = features.shape[0]
    proj_heads = jnp.dot(features, w_in_flat, preferred_element_type=jnp.float32).reshape(
        group_rows, heads_here, in_width
    )
    proj_keys = jnp.dot(features, key_low, preferred_element_type=jnp.float32)

    def mixing(heads_in, keys_in, params_in, taps_in):
        return local_mix(heads_in, keys_in, params_in, taps_in, seq_length)

    gated_mix, mix_pullback = jax.vjp(mixing, proj_heads, proj_keys, head_small, key_taps)
    gain_mix = head_small[:, 0, :]
    square_rows = jnp.sum(gated_mix * gated_mix, axis=(1, 2))
    square_total = lax.psum(square_rows, "mp")
    scale_mix = lax.rsqrt(square_total / (H * P_SIZE) + NORM_EPS)[:, None, None]
    normal_mix = gated_mix * scale_mix
    result_low = (
        (normal_mix * gain_mix[None]).astype(jnp.bfloat16).reshape(group_rows, heads_here * P_SIZE)
    )
    rows_in = result_low
    branch_out = lax.psum_scatter(
        jnp.dot(rows_in, w_out_flat, preferred_element_type=jnp.float32),
        "mp",
        scatter_dimension=0,
        tiled=True,
    )
    hidden_out = (hidden + branch_out).astype(jnp.bfloat16)
    grad_full = lax.all_gather(out_grad, "mp", axis=0, tiled=True)
    out_weight_grad = lax.dot_general(
        result_low, grad_full, (((0,), (0,)), ((), ())), preferred_element_type=jnp.float32
    )
    result_grad = lax.dot_general(
        grad_full, w_out_flat, (((1,), (1,)), ((), ())), preferred_element_type=jnp.float32
    ).reshape(group_rows, heads_here, P_SIZE)
    gain_mix_grad = jnp.sum(result_grad * normal_mix, axis=0)
    normal_grad = result_grad * gain_mix[None]
    cross_rows = jnp.sum(normal_grad * gated_mix, axis=(1, 2))
    cross_total = lax.psum(cross_rows, "mp")
    gated_grad = (
        scale_mix * normal_grad
        - gated_mix * scale_mix**3 * (cross_total / (H * P_SIZE))[:, None, None]
    )
    heads_grad, keys_grad, params_grad, taps_grad = mix_pullback(gated_grad)
    params_grad = params_grad.at[:, 0, :].add(gain_mix_grad)
    heads_low = heads_grad.reshape(group_rows, heads_here * in_width).astype(jnp.bfloat16)
    keys_own = lax.psum_scatter(keys_grad, "mp", scatter_dimension=0, tiled=True)
    keys_low = keys_own.astype(jnp.bfloat16)
    in_weight_grad = lax.dot_general(
        features, heads_low, (((0,), (0,)), ((), ())), preferred_element_type=jnp.float32
    )
    in_weight_grad = jnp.transpose(in_weight_grad.reshape(D, heads_here, in_width), (1, 0, 2))
    block_grad = jnp.concatenate(
        [in_weight_grad, jnp.transpose(out_weight_grad.reshape(heads_here, P_SIZE, D), (0, 2, 1))],
        axis=2,
    )
    key_weight_grad = lax.dot_general(
        normed_low, keys_low, (((0,), (0,)), ((), ())), preferred_element_type=jnp.float32
    )
    rows_in = heads_low
    normed_grad = lax.psum_scatter(
        lax.dot_general(
            rows_in, w_in_flat, (((1,), (1,)), ((), ())), preferred_element_type=jnp.float32
        ),
        "mp",
        scatter_dimension=0,
        tiled=True,
    )
    normed_grad = normed_grad + lax.dot_general(
        keys_low, key_low, (((1,), (1,)), ((), ())), preferred_element_type=jnp.float32
    )
    gain_in_grad = jnp.sum(normed_grad * hidden * scale_in, axis=0)
    scaled_in = normed_grad * gain_in
    cross_in = jnp.sum(scaled_in * hidden, axis=1, keepdims=True)
    hidden_grad = (
        out_grad.astype(jnp.float32) + scale_in * scaled_in - hidden * scale_in**3 * cross_in / D
    )
    shared_grad = jnp.concatenate([taps_grad, gain_in_grad.reshape(-1, taps_grad.shape[1])], axis=0)
    block_total, params_total = lax.psum((block_grad, params_grad), "dp")
    key_total, shared_total = lax.psum((key_weight_grad, shared_grad), ("dp", "mp"))
    head_new = adamw_update(head_small, params_total, head_first, head_second, head_ema, SMALL_RATE)
    key_new = adamw_update(bc_weight, key_total, bc_first, bc_second, bc_ema, MATRIX_RATE)
    shared_new = adamw_update(
        shared_small, shared_total, shared_first, shared_second, shared_ema, SMALL_RATE
    )
    owned_mask = (owners_here == dp_index).astype(jnp.float32)
    own_grad = jnp.tensordot(owned_mask, block_total, axes=1)
    is_owner = jnp.sum(owned_mask) > 0.5
    previous_all = (block_master[0, 0], block_first[0, 0], block_second[0, 0], block_ema[0, 0])
    slot_new = adamw_update(
        previous_all[0], own_grad, previous_all[1], previous_all[2], previous_all[3], MATRIX_RATE
    )
    slot_outs = [
        jnp.where(is_owner, renewed, previous)[None, None]
        for renewed, previous in zip(slot_new, previous_all)
    ]
    return (
        hidden_out,
        hidden_grad,
        slot_outs[0],
        slot_outs[1],
        slot_outs[2],
        slot_outs[3],
        head_new[0],
        head_new[1],
        head_new[2],
        head_new[3],
        key_new[0],
        key_new[1],
        key_new[2],
        key_new[3],
        shared_new[0],
        shared_new[1],
        shared_new[2],
        shared_new[3],
    )


def solution(mesh):
    placed = (
        P(("dp", "mp"), None),
        P(("dp", "mp"), None),
        P("dp"),
        P(),
        P("mp", "dp", None, None),
        P("mp", "dp", None, None),
        P("mp", "dp", None, None),
        P("mp", "dp", None, None),
        P("mp", None, None),
        P("mp", None, None),
        P("mp", None, None),
        P("mp", None, None),
        P(),
        P(),
        P(),
        P(),
        P(),
        P(),
        P(),
        P(),
    )
    return jax.shard_map(
        local,
        mesh=mesh,
        in_specs=placed,
        out_specs=(
            P(("dp", "mp"), None),
            P(("dp", "mp"), None),
            P("mp", "dp", None, None),
            P("mp", "dp", None, None),
            P("mp", "dp", None, None),
            P("mp", "dp", None, None),
            P("mp", None, None),
            P("mp", None, None),
            P("mp", None, None),
            P("mp", None, None),
            P(),
            P(),
            P(),
            P(),
            P(),
            P(),
            P(),
            P(),
        ),
        check_vma=False,
    )
```

profile of v0, /device:TPU:0, one launch (start us, length us, event | category | flops | bytes accessed | tf_op | source)
XLA Modules:
  0.0 1658.8 jit_solution(6648036908415490787)
XLA Ops:
  21.4 45.3 %all-gather.9.cloned.1.call-done = bf16[8,1,768,194]{2,3,1,0:T(8,128)(2,1)} async-done(((bf16[1,1,768,194]{2,3,1,0:T(8,128)(2,1)}), bf16[8,1,768,194]{2,3,1,0:T(8,128)(2,1)}) %all-gather.9.cloned.1.call-update) | async-done | bytes 2383888 | tf_op jit(solution)/shard_map/all_gather | solution.py:160
  74.7 39.1 %all-gather.5.cloned.1.call-done = bf16[4096,768]{1,0:T(8,128)(2,1)} async-done(((bf16[1024,768]{1,0:T(8,128)(2,1)}), bf16[4096,768]{1,0:T(8,128)(2,1)}) %all-gather.5.cloned.1.call-update) | async-done | bytes 6291472 | tf_op jit(solution)/shard_map/all_gather | solution.py:171
  118.6 8.9 fusion.121
  132.1 13.7 rev.33
  145.7 7.9 fusion.88
  173.2 29.2 %fusion.98 = (f32[4096,384]{0,1:T(8,128)}, f32[4096,384]{0,1:T(8,128)}) fusion(f32[384]{0:T(512)S(1)} %mul.996, pred[4096]{0:T(1024)(128)(4,1)S(1)} %get-tuple-element.1093, f32[384]{0:T(512)S(1)} %mul.993, pred[4096]{0:T(1024)(128)(4,1)S(1)} %get-tuple-element.1094, f32[384]{0:T(512)S(1)} %mul.990, pred[4096]{0:T(1024)(128)(4,1)S(1)} %get-tuple-element.1095, ...), kind=kLoop, calls=%fused_computation.187 | loop fusion | flops 37748736 | bytes 18913792 | tf_op jit(solution)/shard_map/jvp(jit(silu))/mul | solution.py:97
  202.5 20.0 %rev.30 = f32[4096,6,64]{0,2,1:T(8,128)} reverse(f32[4096,6,64]{0,2,1:T(8,128)} %bitcast.605), dimensions={0} | reverse | bytes 12582912 | tf_op jit(solution)/shard_map/jvp()/rev | solution.py:113
  222.5 9.0 fusion.169
  233.5 60.7 %while.74 = (s32[]{:T(128)}, f32[6,64,64]{2,1,0:T(8,128)S(1)}, f32[16,6,64,64]{3,2,1,0:T(8,128)}, f32[16,6]{1,0:T(8,128)S(1)}, f32[16,6,1,1]{1,3,2,0:T(1,128)S(1...) while((s32[]{:T(128)}, f32[6,64,64]{2,1,0:T(8,128)S(1)}, ...), condition=%wide.region_8.9_spmd.clone, body=%wide.region_7.8_spmd.clone.sunk | while | flops 147459 | bytes 985312 | solution.py:79
  303.2 11.0 fusion.166
  316.3 60.5 %while.73 = (s32[]{:T(128)}, f32[6,64,64]{2,1,0:T(8,128)S(1)}, f32[16,6,64,64]{3,2,1,0:T(8,128)}, f32[16,6]{1,0:T(8,128)S(1)}, f32[16,6,1,1]{1,3,2,0:T(1,128)S(1...) while((s32[]{:T(128)}, f32[6,64,64]{2,1,0:T(8,128)S(1)}, ...), condition=%wide.region_4.5_spmd.clone, body=%wide.region_3.4_spmd.clone.sunk | while | flops 147459 | bytes 985312 | solution.py:79
  376.9 16.5 rev.32
  411.2 29.6 %fusion.84 = f32[16,6,8,8,256]{4,3,2,1,0:T(8,128)S(1)} fusion(f32[16,256,6,64]{1,3,2,0:T(8,128)S(1)} %bitcast.666, f32[16,256,6]{1,2,0:T(8,128)S(1)} %get-tuple-element.1065, f32[16,6,256]{2,1,0:T(8,128)S(1)} %copy.611, f32[16,256,256]{2,1,0:T(8,128)S(1)} %fusion.278, f32[16,6,256]{2,1,0:T(8,128)S(1)} %get-tuple-element.1064, ...), kind=kOutput, calls=%fused_computation.144 | convolution fusion | flops 4866441216 | bytes 23429120 | tf_op jit(solution)/shard_map/jvp(bhij,bjhp->bihp)/dot_general | solution.py:52
  446.0 20.1 %rev.34 = f32[4096,6,64]{0,2,1:T(8,128)} reverse(f32[4096,6,64]{0,2,1:T(8,128)} %pad_select_fusion), dimensions={0} | reverse | bytes 12582912 | tf_op jit(solution)/shard_map/jvp()/rev | solution.py:111
  469.7 8.0 fusion.276
  477.7 7.1 fusion.277
  484.8 34.4 %fusion.85 = f32[16,6,8,8,256]{4,3,2,1,0:T(8,128)} fusion(f32[16,256,6,64]{1,3,2,0:T(8,128)} %bitcast.668, f32[16,256,6]{1,2,0:T(8,128)S(1)} %get-tuple-element.1063, f32[16,6,256]{2,1,0:T(8,128)S(1)} %copy.593, f32[16,256,256]{2,1,0:T(8,128)} %fusion.276, f32[16,6,256]{2,1,0:T(8,128)S(1)} %get-tuple-element.1062, pred[256,256]{1,0:T(8,128)(4,1)S(1)} %copy-done.79, ...), kind=kOutput, calls=%fused_computation.146 | convolution fusion | flops 4866441216 | bytes 23429120 | tf_op jit(solution)/shard_map/jvp(bhij,bjhp->bihp)/dot_general | solution.py:52
  519.2 6.3 copy.785
  525.5 9.0 multiply_reduce_fusion.16
  534.6 10.2 psum.42
  552.6 10.1 psum.43
  562.7 17.4 %multiply_reduce_fusion.14 = (f32[6,64]{1,0:T(8,128)}, f32[4096,6,64]{0,2,1:T(8,128)}, f32[4096,6,64]{0,2,1:T(8,128)}) fusion(f32[4096,6,64]{0,2,1:T(8,128)} %bitcast.607, f32[4096,6,130]{0,2,1:T(8,128)} %copy-done.20, f32[4096]{0:T(1024)S(1)} %broadcast_multiply_fusion.1, f32[4096,6,64]{0,2,1:T(8,128)} %get-tuple-element.1013, ...), kind=kLoop, calls=%fused_computation.164 | loop fusion | flops 29884032 | bytes 44092416 | tf_op jit(solution)/shard_map/transpose(jvp())/reduce_sum | solution.py:117
  580.1 20.4 %rev.35 = f32[4096,6,64]{0,2,1:T(8,128)} reverse(f32[4096,6,64]{0,2,1:T(8,128)} %get-tuple-element.1008), dimensions={0} | reverse | bytes 12582912 | tf_op jit(solution)/shard_map/transpose(jvp())/rev | solution.py:111
  600.6 12.5 slice_select_fusion.1
  639.5 7.5 fusion.164
  649.1 76.9 %while.76 = (s32[]{:T(128)}, f32[6,64,64]{2,1,0:T(8,128)S(1)}, f32[16,6,64,64]{3,2,1,0:T(8,128)}, f32[16,6]{1,0:T(8,128)S(1)}, f32[16,6,64,64]{2,3,1,0:T(8,128)}...) while((s32[]{:T(128)}, f32[6,64,64]{2,1,0:T(8,128)S(1)}, ...), condition=%wide.region_28.29_spmd.clone, body=%wide.region_26.28_spmd.clone.sunk | while | flops 172036 | bytes 1081748 | solution.py:79
  726.7 8.4 copy.797
  736.5 8.3 copy.795
  744.9 7.8 fusion.165
  754.8 87.2 %while.75 = (s32[]{:T(128)}, f32[6,64,64]{2,1,0:T(8,128)S(1)}, f32[16,6,64,64]{3,2,1,0:T(8,128)}, f32[16,6]{1,0:T(8,128)S(1)}, f32[16,6,64,64]{2,3,1,0:T(8,128)}...) while((s32[]{:T(128)}, f32[6,64,64]{2,1,0:T(8,128)S(1)}, ...), condition=%wide.region_16.17_spmd.clone, body=%wide.region_14.16_spmd.clone.sunk | while | flops 172036 | bytes 1081748 | solution.py:79
  842.2 8.3 copy.796
  859.5 7.3 fusion.281
  866.8 11.9 multiply_reduce_fusion.5
  879.7 8.0 fusion.282
  887.7 11.6 multiply_reduce_fusion.4
  900.3 35.2 %fusion.79 = f32[16,6,256,256]{3,2,1,0:T(8,128)} fusion(f32[16,256,6,64]{1,0,3,2:T(8,128)} %bitcast.598, f32[16,256,6,64]{1,0,3,2:T(8,128)} %bitcast.655), kind=kOutput, calls=%fused_computation.138 | convolution fusion | flops 4831838208 | bytes 37748736 | tf_op jit(solution)/shard_map/transpose(jvp(jvp()))/checkpoint/bhij,bjhp->bihp/dot_general | solution.py:52
  935.6 66.6 %fusion.35 = (f32[16,6,256]{2,1,0:T(8,128)}, f32[16,6,256]{2,1,0:T(8,128)}, f32[16,6,256]{2,1,0:T(8,128)}, f32[16,256,256]{2,1,0:T(8,128)}, f32[16,256,256]{2,1,...) fusion(f32[16,6,256]{2,1,0:T(8,128)S(1)} %bitcast.704, ...), kind=kOutput, calls=%fused_computation.67 | convolution fusion | flops 5018337280 | bytes 55574528 | tf_op jit(solution)/shard_map/transpose(jvp(jvp()))/checkpoint/bhij,bjhp->bihp/dot_general | solution.py:52
  1003.4 9.1 fusion.185
  1012.5 26.9 %fusion.76 = f32[16,6,8,8,256]{4,3,2,1,0:T(8,128)} fusion(f32[16,256,6,64]{1,3,2,0:T(8,128)S(1)} %copy-done.38, f32[16,256,6]{1,2,0:T(8,128)S(1)} %get-tuple-element.1055, f32[16,6,256]{2,1,0:T(8,128)S(1)} %bitcast.703, f32[16,256,256]{2,1,0:T(8,128)} %fusion.282, f32[16,6,256]{2,1,0:T(8,128)S(1)} %copy-done.76, pred[256,256]{1,0:T(8,128)(4,1)S(1)} %copy-done.80, ...), kind=kOutput, calls=%fused_computation.134 | convolution fusion | flops 4866441216 | bytes 23429120 | tf_op jit(solution)/shard_map/transpose(jvp(jvp()))/checkpoint/bhij,bjhp->bihp/dot_general | solution.py:52
  1050.2 7.3 copy.791
  1058.3 8.6 fusion.180
  1067.0 26.3 %fusion.77 = f32[16,6,8,8,256]{4,3,2,1,0:T(8,128)} fusion(f32[16,256,6,64]{1,3,2,0:T(8,128)S(1)} %bitcast.682, f32[16,256,6]{1,2,0:T(8,128)S(1)} %get-tuple-element.1053, f32[16,6,256]{2,1,0:T(8,128)S(1)} %bitcast.705, f32[16,256,256]{2,1,0:T(8,128)S(1)} %copy-done.41, f32[16,6,256]{2,1,0:T(8,128)S(1)} %copy-done.75, pred[256,256]{1,0:T(8,128)(4,1)S(1)} %copy-done.80, ...), kind=kOutput, calls=%fused_computation.136 | convolution fusion | flops 4866441216 | bytes 23429120 | tf_op jit(solution)/shard_map/transpose(jvp(jvp()))/checkpoint/bhij,bjhp->bihp/dot_general | solution.py:52
  1108.8 20.0 %rev.37 = f32[4096,6,64]{0,2,1:T(8,128)} reverse(f32[4096,6,64]{0,2,1:T(8,128)} %bitcast.665), dimensions={0} | reverse | bytes 12582912 | tf_op jit(solution)/shard_map/transpose(jvp())/rev | solution.py:113
  1128.8 14.9 reduce-window.50
  1144.1 14.9 reduce-window.56
  1161.1 10.3 rev.39
  1176.5 10.1 rev.38
  1187.4 19.2 %multiply_reduce_fusion.23 = (f32[256]{0:T(256)}, f32[256]{0:T(256)}, f32[256]{0:T(256)}, f32[256]{0:T(256)}, f32[256]{0:T(256)}, /*index=5*/f32[256]{0:T(256)}, f32[256]{0:T(256)}, f32[4096,256]{1,0:T(8,128)S(1)}) fusion(f32[4096,256]{1,0:T(8,128)} %copy-done.13, pred[4096]{0:T(1024)(128)(4,1)S(1)} %copy-done.58, pred[4096]{0:T(1024)(128)(4,1)S(1)} %copy-done.64, ...), kind=kLoop, calls=%fused_computation.229 | loop fusion | flops 34601216 | bytes 16813056 | tf_op jit(solution)/shard_map/transpose(jvp())/reduce_sum | solution.py:34
  1206.6 6.4 multiply_select_fusion.15
  1213.0 6.5 pad_add_fusion.6
  1226.7 13.5 add_add_fusion
  1240.2 16.0 multiply_reduce_fusion.13
  1256.3 16.6 multiply_select_fusion.8
  1272.9 20.8 %pad_add_fusion = f32[4096,384]{0,1:T(8,128)} fusion(f32[4096,384]{0,1:T(8,128)} %get-tuple-element.1031, f32[4096,384]{0,1:T(8,128)} %get-tuple-element.1032, f32[4096,384]{0,1:T(8,128)} %get-tuple-element.1033, f32[4096,384]{0,1:T(8,128)} %get-tuple-element.1034, f32[4096,384]{0,1:T(8,128)} %get-tuple-element.1035, f32[4096,384]{0,1:T(8,128)} %get-tuple-element.1036, ...), kind=kLoop, calls=%fused_computation.121 | loop fusion | flops 9437184 | bytes 50331648 | tf_op jit(solution)/shard_map/transpose(jvp())/add_any | solution.py:32
  1293.7 9.2 add_convert_fusion
  1305.7 12.4 convolution_bitcast_fusion
  1318.8 10.9 convolution_bitcast_fusion.1
  1331.7 9.1 convert_element_type.65
  1341.0 9.0 dot_general.202
  1350.0 6.9 fusion.173
  1365.8 152.4 %all-reduce.55 = (bf16[6,768,194]{1,2,0:T(8,128)(2,1)S(1)}, f32[6,10,64]{2,0,1:T(8,128)}) all-reduce(f32[6,768,194]{1,2,0:T(8,128)} %pad_maximum_fusion, f32[6,10,64]{2,0,1:T(8,128)S(1)} %fusion.243), channel_id=1, replica_groups=mesh['dp'=8,'mp'=4] {'dp'}, use_global_device_ids=true, to_apply=%region_44.45 | all-reduce | flops 897792 | bytes 5394432 | tf_op jit(solution)/shard_map/psum | solution.py:248
  1518.2 27.8 %fusion.117 = f32[1,768,194]{0,1,2:T(8,128)} fusion(bf16[6,768,194]{1,2,0:T(8,128)(2,1)S(1)} %get-tuple-element.986, s32[]{:T(128)S(6)} %axis_index.25, s32[24]{0:T(128)S(1)} %copy-done.135, s32[]{:T(128)S(6)} %select_n.236), kind=kOutput, calls=%fused_computation.213 | convolution fusion | flops 1787910 | bytes 2383976 | tf_op jit(solution)/shard_map/dot_general | solution.py:256
  1546.0 44.1 %copy.735 = f32[1,768,194]{1,2,0:T(8,128)S(1)} copy(f32[1,768,194]{0,1,2:T(8,128)} %fusion.117) | data formatting | bytes 1191936 | tf_op jit(solution)/shard_map/dot_general | solution.py:256
  1607.1 38.6 %psum.47 = f32[10,256]{1,0:T(8,128)S(1)} all-reduce(f32[10,256]{1,0:T(8,128)S(1)} %pad_maximum_fusion.1), channel_id=1, replica_groups=mesh['dp'=8,'mp'=4] {'dp','mp'}, use_global_device_ids=true, to_apply=%region_65.66 | all-reduce | flops 2560 | bytes 20480 | tf_op jit(solution)/shard_map/psum | solution.py:249
  (1047 shorter events, 504.1 us)
Async XLA Ops:
  7.2 59.5 %all-gather.9.cloned.1.call-start = ((), (), s32[]{:S(2)}) async-start(), calls=%async_computation.9 | async-start | bytes 2764800 | tf_op jit(solution)/shard_map/all_gather | solution.py:160
  9.1 104.7 %all-gather.5.cloned.1.call-start = ((), (), s32[]{:S(2)}) async-start(), calls=%async_computation.3 | async-start | bytes 7864320 | tf_op jit(solution)/shard_map/all_gather | solution.py:171
  9.9 56.9 %copy-start.83 = (f32[768]{0:T(1024)}, f32[768]{0:T(1024)S(1)}, u32[]{:S(2)}) copy-start(f32[768]{0:T(1024)S(1)} %mul.974) | copy-start | bytes 9220
  15.9 528.9 %all-gather.7.cloned.1.call-start = ((), (), s32[]{:S(2)}) async-start(), calls=%async_computation.5 | async-start | bytes 7864320 | tf_op jit(solution)/shard_map/all_gather | solution.py:198
  16.6 1286.3 %reduce-scatter.8.cloned.1.call-start = ((), (), s32[]{:S(2)}) async-start(), calls=%async_computation.7 | async-start | bytes 5242880 | tf_op jit(solution)/shard_map/reduce_scatter | solution.py:216
  17.6 100.9 %copy-start.118 = (f32[1,256]{1,0:T(1,128)}, f32[1,256]{1,0:T(1,128)S(1)}, u32[]{:S(2)}) copy-start(f32[1,256]{1,0:T(1,128)S(1)} %get-tuple-element.1077) | copy-start | bytes 3076
  17.6 100.9 %copy-start.120 = (f32[1,256]{1,0:T(1,128)}, f32[1,256]{1,0:T(1,128)S(1)}, u32[]{:S(2)}) copy-start(f32[1,256]{1,0:T(1,128)S(1)} %get-tuple-element.1078) | copy-start | bytes 3076
  17.6 100.9 %copy-start.122 = (f32[1,256]{1,0:T(1,128)}, f32[1,256]{1,0:T(1,128)S(1)}, u32[]{:S(2)}) copy-start(f32[1,256]{1,0:T(1,128)S(1)} %get-tuple-element.1079) | copy-start | bytes 3076
  17.7 100.9 %copy-start.124 = (f32[1,256]{1,0:T(1,128)}, f32[1,256]{1,0:T(1,128)S(1)}, u32[]{:S(2)}) copy-start(f32[1,256]{1,0:T(1,128)S(1)} %get-tuple-element.1080) | copy-start | bytes 3076
  17.7 100.9 %copy-start.126 = (f32[1,256]{1,0:T(1,128)}, f32[1,256]{1,0:T(1,128)S(1)}, u32[]{:S(2)}) copy-start(f32[1,256]{1,0:T(1,128)S(1)} %get-tuple-element.1081) | copy-start | bytes 3076
  17.7 100.9 %copy-start.128 = (f32[1,256]{1,0:T(1,128)}, f32[1,256]{1,0:T(1,128)S(1)}, u32[]{:S(2)}) copy-start(f32[1,256]{1,0:T(1,128)S(1)} %get-tuple-element.1082) | copy-start | bytes 3076
  17.7 100.9 %copy-start.130 = (f32[1,256]{1,0:T(1,128)}, f32[1,256]{1,0:T(1,128)S(1)}, u32[]{:S(2)}) copy-start(f32[1,256]{1,0:T(1,128)S(1)} %get-tuple-element.1083) | copy-start | bytes 3076
  17.7 139.2 %copy-start.90 = (f32[6,2]{1,0:T(8,128)}, f32[6,2]{1,0:T(8,128)S(1)}, u32[]{:S(2)}) copy-start(f32[6,2]{1,0:T(8,128)S(1)} %slice_bitcast_fusion.4) | copy-start | bytes 148
  17.7 507.8 %copy-start.94 = (f32[6,64]{1,0:T(8,128)}, f32[6,64]{1,0:T(8,128)S(1)}, u32[]{:S(2)}) copy-start(f32[6,64]{1,0:T(8,128)S(1)} %get-tuple-element.1067) | copy-start | bytes 4612
  17.7 545.0 %copy-start.92 = (f32[6,64]{1,0:T(8,128)}, f32[6,64]{1,0:T(8,128)S(1)}, u32[]{:S(2)}) copy-start(f32[6,64]{1,0:T(8,128)S(1)} %get-tuple-element.1066) | copy-start | bytes 4612
  19.5 153.6 %copy-start.53 = (pred[4096]{0:T(1024)(128)(4,1)}, pred[4096]{0:T(1024)(128)(4,1)S(1)}, u32[]{:S(2)}) copy-start(pred[4096]{0:T(1024)(128)(4,1)S(1)} %get-tuple-element.1095) | copy-start | bytes 12292
  19.5 153.6 %copy-start.55 = (pred[4096]{0:T(1024)(128)(4,1)}, pred[4096]{0:T(1024)(128)(4,1)S(1)}, u32[]{:S(2)}) copy-start(pred[4096]{0:T(1024)(128)(4,1)S(1)} %get-tuple-element.1096) | copy-start | bytes 12292
  19.7 153.4 %copy-start.57 = (pred[4096]{0:T(1024)(128)(4,1)}, pred[4096]{0:T(1024)(128)(4,1)S(1)}, u32[]{:S(2)}) copy-start(pred[4096]{0:T(1024)(128)(4,1)S(1)} %get-tuple-element.1093) | copy-start | bytes 12292
  19.8 153.4 %copy-start.59 = (pred[4096]{0:T(1024)(128)(4,1)}, pred[4096]{0:T(1024)(128)(4,1)S(1)}, u32[]{:S(2)}) copy-start(pred[4096]{0:T(1024)(128)(4,1)S(1)} %get-tuple-element.1094) | copy-start | bytes 12292
  20.0 153.2 %copy-start.61 = (pred[4096]{0:T(1024)(128)(4,1)}, pred[4096]{0:T(1024)(128)(4,1)S(1)}, u32[]{:S(2)}) copy-start(pred[4096]{0:T(1024)(128)(4,1)S(1)} %get-tuple-element.1097) | copy-start | bytes 12292
  20.0 153.2 %copy-start.63 = (pred[4096]{0:T(1024)(128)(4,1)}, pred[4096]{0:T(1024)(128)(4,1)S(1)}, u32[]{:S(2)}) copy-start(pred[4096]{0:T(1024)(128)(4,1)S(1)} %get-tuple-element.1098) | copy-start | bytes 12292
  20.2 153.0 %copy-start.65 = (pred[4096]{0:T(1024)(128)(4,1)}, pred[4096]{0:T(1024)(128)(4,1)S(1)}, u32[]{:S(2)}) copy-start(pred[4096]{0:T(1024)(128)(4,1)S(1)} %get-tuple-element.1100) | copy-start | bytes 12292
  21.0 152.2 %copy-start.96 = (f32[384]{0:T(512)}, f32[384]{0:T(512)S(1)}, u32[]{:S(2)}) copy-start(f32[384]{0:T(512)S(1)} %mul.978) | copy-start | bytes 4612
  21.0 152.1 %copy-start.98 = (f32[384]{0:T(512)}, f32[384]{0:T(512)S(1)}, u32[]{:S(2)}) copy-start(f32[384]{0:T(512)S(1)} %mul.996) | copy-start | bytes 4612
  21.1 152.1 %copy-start.100 = (f32[384]{0:T(512)}, f32[384]{0:T(512)S(1)}, u32[]{:S(2)}) copy-start(f32[384]{0:T(512)S(1)} %mul.993) | copy-start | bytes 4612
  21.2 152.0 %copy-start.102 = (f32[384]{0:T(512)}, f32[384]{0:T(512)S(1)}, u32[]{:S(2)}) copy-start(f32[384]{0:T(512)S(1)} %mul.990) | copy-start | bytes 4612
  21.3 151.9 %copy-start.104 = (f32[384]{0:T(512)}, f32[384]{0:T(512)S(1)}, u32[]{:S(2)}) copy-start(f32[384]{0:T(512)S(1)} %mul.987) | copy-start | bytes 4612
  21.4 151.9 %copy-start.106 = (f32[384]{0:T(512)}, f32[384]{0:T(512)S(1)}, u32[]{:S(2)}) copy-start(f32[384]{0:T(512)S(1)} %mul.984) | copy-start | bytes 4612
  21.4 151.8 %copy-start.108 = (f32[384]{0:T(512)}, f32[384]{0:T(512)S(1)}, u32[]{:S(2)}) copy-start(f32[384]{0:T(512)S(1)} %mul.981) | copy-start | bytes 4612
  69.1 44.7 %copy-start.35 = (f32[768,256]{1,0:T(8,128)S(1)}, f32[768,256]{1,0:T(8,128)}, u32[]{:S(2)}) copy-start(f32[768,256]{1,0:T(8,128)} %param.42) | copy-start | bytes 2359300
  376.8 26.0 %copy-start.133 = (f32[16,6,1,1]{1,3,2,0:T(1,128)}, f32[16,6,1,1]{1,3,2,0:T(1,128)S(1)}, u32[]{:S(2)}) copy-start(f32[16,6,1,1]{1,3,2,0:T(1,128)S(1)} %get-tuple-element.1390) | copy-start | bytes 1156
  477.7 47.8 %slice-start.4 = ((s8[6291456]{0:T(1024)(128)(4,1)}), s8[4194304]{0:T(1024)(128)(4,1)S(1)}, s32[]{:S(2)}) async-start(s8[6291456]{0:T(1024)(128)(4,1)} %bitcast.608), calls=%async_computation.14 | async-start | bytes 8388608
  477.7 47.8 %slice-start.14 = ((s8[6291456]{0:T(1024)(128)(4,1)}), s8[4194304]{0:T(1024)(128)(4,1)S(1)}, s32[]{:S(2)}) async-start(s8[6291456]{0:T(1024)(128)(4,1)} %bitcast.658), calls=%async_computation.24 | async-start | bytes 8388608
  484.8 40.7 %slice-start.5 = ((s8[6291456]{0:T(1024)(128)(4,1)}), s8[2097152]{0:T(1024)(128)(4,1)S(1)}, s32[]{:S(2)}) async-start(s8[6291456]{0:T(1024)(128)(4,1)} %bitcast.608), calls=%async_computation.15 | async-start | bytes 4194304
  484.8 40.7 %slice-start.15 = ((s8[6291456]{0:T(1024)(128)(4,1)}), s8[2097152]{0:T(1024)(128)(4,1)S(1)}, s32[]{:S(2)}) async-start(s8[6291456]{0:T(1024)(128)(4,1)} %bitcast.658), calls=%async_computation.25 | async-start | bytes 4194304
  580.1 20.4 %copy-start.116 = (pred[4095]{0:T(1024)(128)(4,1)S(1)}, pred[4095]{0:T(1024)(128)(4,1)}, u32[]{:S(2)}) copy-start(pred[4095]{0:T(1024)(128)(4,1)} %slice.312) | copy-start | bytes 12289
  855.1 147.1 %copy-start.46 = (f32[16,6,256]{2,0,1:T(8,128)}, f32[16,6,256]{2,0,1:T(8,128)S(1)}, u32[]{:S(2)}) copy-start(f32[16,6,256]{2,0,1:T(8,128)S(1)} %copy_bitcast_fusion.4) | copy-start | bytes 294916
  900.3 35.2 %copy-start.72 = (f32[16,256,6]{1,2,0:T(8,128)S(1)}, f32[16,256,6]{1,2,0:T(8,128)}, u32[]{:S(2)}) copy-start(f32[16,256,6]{1,2,0:T(8,128)} %copy.964) | copy-start | bytes 294916
  900.3 35.2 %copy-start.73 = (f32[16,256,6]{1,2,0:T(8,128)S(1)}, f32[16,256,6]{1,2,0:T(8,128)}, u32[]{:S(2)}) copy-start(f32[16,256,6]{1,2,0:T(8,128)} %copy.965) | copy-start | bytes 294916
  900.3 35.2 %copy-start.80 = (pred[256,256]{1,0:T(8,128)(4,1)S(1)}, pred[256,256]{1,0:T(8,128)(4,1)}, u32[]{:S(2)}) copy-start(pred[256,256]{1,0:T(8,128)(4,1)} %iota_compare_fusion) | copy-start | bytes 196612
  935.5 67.8 %slice-start.2 = ((s8[6291456]{0:T(1024)(128)(4,1)}), s8[4194304]{0:T(1024)(128)(4,1)S(1)}, s32[]{:S(2)}) async-start(s8[6291456]{0:T(1024)(128)(4,1)} %bitcast.602), calls=%async_computation.12 | async-start | bytes 8388608
  935.5 66.6 %copy-start.51 = (f32[16,6,256]{2,1,0:T(8,128)S(1)}, f32[16,6,256]{2,1,0:T(8,128)}, u32[]{:S(2)}) copy-start(f32[16,6,256]{2,1,0:T(8,128)} %fusion.207) | copy-start | bytes 294916
  935.5 67.8 %slice-start.3 = ((s8[6291456]{0:T(1024)(128)(4,1)}), s8[2097152]{0:T(1024)(128)(4,1)S(1)}, s32[]{:S(2)}) async-start(s8[6291456]{0:T(1024)(128)(4,1)} %bitcast.602), calls=%async_computation.13 | async-start | bytes 4194304
  935.5 67.8 %copy-start.15 = (f32[16,6,64,64]{3,2,1,0:T(8,128)S(1)}, f32[16,6,64,64]{3,2,1,0:T(8,128)}, u32[]{:S(2)}) copy-start(f32[16,6,64,64]{3,2,1,0:T(8,128)} %get-tuple-element.512) | copy-start | bytes 4718596
  1012.5 27.0 %copy-start.8 = (f32[4096,64]{1,0:T(8,128)S(1)}, f32[4096,64]{1,0:T(8,128)}, u32[]{:S(2)}) copy-start(f32[4096,64]{1,0:T(8,128)} %get-tuple-element.1044) | copy-start | bytes 3145732
  1012.5 27.0 %copy-start.30 = (f32[16,256,256]{2,1,0:T(8,128)S(1)}, f32[16,256,256]{2,1,0:T(8,128)}, u32[]{:S(2)}) copy-start(f32[16,256,256]{2,1,0:T(8,128)} %get-tuple-element.914) | copy-start | bytes 12582916
  1012.5 27.0 %copy-start.44 = (f32[16,256,64]{1,2,0:T(8,128)S(1)}, f32[16,256,64]{1,2,0:T(8,128)}, u32[]{:S(2)}) copy-start(f32[16,256,64]{1,2,0:T(8,128)} %fusion.178) | copy-start | bytes 3145732
  1067.0 26.4 %copy-start.29 = (f32[16,256,256]{2,1,0:T(8,128)S(1)}, f32[16,256,256]{2,1,0:T(8,128)}, u32[]{:S(2)}) copy-start(f32[16,256,256]{2,1,0:T(8,128)} %get-tuple-element.895) | copy-start | bytes 12582916
  1067.0 26.4 %copy-start.43 = (f32[16,256,64]{1,2,0:T(8,128)S(1)}, f32[16,256,64]{1,2,0:T(8,128)}, u32[]{:S(2)}) copy-start(f32[16,256,64]{1,2,0:T(8,128)} %fusion.179) | copy-start | bytes 3145732
  1108.8 35.3 %copy-start.52 = (f32[16,6,2,128]{3,0,1,2:T(8,128)S(1)}, f32[16,6,2,128]{3,0,1,2:T(8,128)}, u32[]{:S(2)}) copy-start(f32[16,6,2,128]{3,0,1,2:T(8,128)} %copy.676) | copy-start | bytes 294916
  1108.8 50.7 %copy-start.47 = (f32[16,6,256]{2,0,1:T(8,128)S(1)}, f32[16,6,256]{2,0,1:T(8,128)}, u32[]{:S(2)}) copy-start(f32[16,6,256]{2,0,1:T(8,128)} %copy-done.46) | copy-start | bytes 294916
  1108.8 50.7 %copy-start.71 = (f32[16,6,256]{2,1,0:T(8,128)S(1)}, f32[16,6,256]{2,1,0:T(8,128)}, u32[]{:S(2)}) copy-start(f32[16,6,256]{2,1,0:T(8,128)} %get-tuple-element.915) | copy-start | bytes 294916
  1219.5 20.7 %slice-start.8 = ((s8[6291456]{0:T(1024)(128)(4,1)}), s8[2097152]{0:T(1024)(128)(4,1)S(1)}, s32[]{:S(2)}) async-start(s8[6291456]{0:T(1024)(128)(4,1)} %bitcast.622), calls=%async_computation.18 | async-start | bytes 4194304
  1219.5 378.4 %all-reduce.54.cloned.1.call-start = ((), (), s32[]{:S(2)}) async-start(), calls=%async_computation.8 | async-start | bytes 1572864 | tf_op jit(solution)/shard_map/psum | solution.py:249
  1272.9 20.8 %copy-start.48 = (f32[4096,6,2]{0,2,1:T(2,128)S(1)}, f32[4096,6,2]{0,2,1:T(2,128)}, u32[]{:S(2)}) copy-start(f32[4096,6,2]{0,2,1:T(2,128)} %get-tuple-element.1010) | copy-start | bytes 589828
  1305.6 296.4 %reduce-scatter.6.cloned.1.call-start = ((), (), s32[]{:S(2)}) async-start(), calls=%async_computation.6 | async-start | bytes 15728640 | tf_op jit(solution)/shard_map/reduce_scatter | solution.py:230
  1318.1 328.3 %reduce-scatter.4.cloned.1.call-start = ((), (), s32[]{:S(2)}) async-start(), calls=%async_computation.4 | async-start | bytes 15728640 | tf_op jit(solution)/shard_map/reduce_scatter | solution.py:191
  1546.0 44.2 %copy-start.40 = (f32[1,1,768,194]{2,1,3,0:T(1,128)S(1)}, f32[1,1,768,194]{2,1,3,0:T(1,128)}, u32[]{:S(2)}) copy-start(f32[1,1,768,194]{2,1,3,0:T(1,128)} %param.34) | copy-start | bytes 1787908
  1546.0 44.2 %copy-start.49 = (f32[1,1,768,194]{2,1,3,0:T(1,128)S(1)}, f32[1,1,768,194]{2,1,3,0:T(1,128)}, u32[]{:S(2)}) copy-start(f32[1,1,768,194]{2,1,3,0:T(1,128)} %param.37) | copy-start | bytes 1787908
  1601.9 43.8 %copy-start.85 = (f32[10,256]{1,0:T(8,128)S(1)}, f32[10,256]{1,0:T(8,128)}, u32[]{:S(2)}) copy-start(f32[10,256]{1,0:T(8,128)} %param.46) | copy-start | bytes 30724
  1601.9 43.8 %copy-start.112 = (f32[10,256]{1,0:T(8,128)S(1)}, f32[10,256]{1,0:T(8,128)}, u32[]{:S(2)}) copy-start(f32[10,256]{1,0:T(8,128)} %param.49) | copy-start | bytes 30724
  1601.9 43.8 %copy-start.113 = (f32[10,256]{1,0:T(8,128)S(1)}, f32[10,256]{1,0:T(8,128)}, u32[]{:S(2)}) copy-start(f32[10,256]{1,0:T(8,128)} %param.47) | copy-start | bytes 30724
  1602.0 43.8 %copy-start.114 = (f32[10,256]{1,0:T(8,128)S(1)}, f32[10,256]{1,0:T(8,128)}, u32[]{:S(2)}) copy-start(f32[10,256]{1,0:T(8,128)} %param.48) | copy-start | bytes 30724
  1602.0 44.4 %copy-start.115 = (f32[1024]{0:T(1024)S(1)}, f32[1024]{0:T(1024)}, u32[]{:S(2)}) copy-start(f32[1024]{0:T(1024)} %get-tuple-element.1084) | copy-start | bytes 12292
  (113 other events, 1064.3 us)
Sparse Core Ops, SparseCore 0:
  10.8 55.9 all-gather.8
  68.9 44.9 all-gather.4
  115.4 46.3 all-gather.6
  1219.6 45.7 reduce-scatter.7
  1305.8 135.6 all-reduce.53
  1443.9 97.4 reduce-scatter.5
  1544.0 99.9 reduce-scatter.3
where the time goes:
time: 1680 us; the launch traced here: 1660 us
  local copies, waits for them, and re-layouts  457 us (27%)
  matrix products  457 us (27%)
  other arithmetic  428 us (25%)
  blocking collectives  211 us (13%)
  waiting for transfers between devices  85.3 us (5%)
  between operations  18.2 us (1%)
    dot_general x6, matrix products, within_blocks(): jnp.einsum('bhij,bjhp->bihp', weights, values_blk, precision=PRECISE)  219 us
    psum x1, blocking collectives, local(): block_total, params_total = lax.psum((block_grad, params_grad), 'dp')  152 us
    dynamic_slice x192, local copies, waits for them, and re-layouts, state_mix(): lax.scan(carry_state, initial, (local_state, log_decay[:, :, -1], keep_fl...  105 us
    dynamic_update_slice x64, other arithmetic, state_mix(): lax.scan(carry_state, initial, (local_state, log_decay[:, :, -1], keep_fl...  65.3 us
    dot_general x6, matrix products, within_blocks(): jnp.einsum('bjn,bhj,bjhp->bhnp', b_blk, tail_decay, values_blk, precision...  61.2 us
    reduce_sum x32, other arithmetic, carry_state(): new_state = entering * jnp.exp(total_decay)[:, None, None] + local_state  54.8 us
    unnamed x347, local copies, waits for them, and re-layouts  52.1 us
    dot_general x8, matrix products, within_blocks(): scores = jnp.einsum('bin,bjn->bij', c_blk, b_blk, precision=PRECISE)  47.9 us
  transfers between devices with their start and end apart: 7, of which 2 were waited for; matrix products, arithmetic and copies ran while one was open for 40% of the time, Pallas kernels for 0%

commit v1 on v0

--- a/solution.py
+++ b/solution.py
@@ -246,7 +246,7 @@
     )
     shared_grad = jnp.concatenate([taps_grad, gain_in_grad.reshape(-1, taps_grad.shape[1])], axis=0)
     block_total, params_total = lax.psum((block_grad, params_grad), "dp")
-    key_total, shared_total = lax.psum((key_weight_grad, shared_grad), ("dp", "mp"))
+    key_total, shared_total = lax.psum(lax.psum((key_weight_grad, shared_grad), "mp"), "dp")
     head_new = adamw_update(head_small, params_total, head_first, head_second, head_ema, SMALL_RATE)
     key_new = adamw_update(bc_weight, key_total, bc_first, bc_second, bc_ema, MATRIX_RATE)
     shared_new = adamw_update(

time: 1680 us -> 1790 us (1.065)
  waiting for transfers between devices: 85.3 us -> 228 us
  blocking collectives: 211 us -> 183 us
    reduce_scatter x1, waiting for transfers between devices: 0.02 us -> 96.8 us  [local(): lax.psum_scatter(lax.dot_general(rows_in, w_in_flat, (((1,), (1,)), ((),...]
    psum x1 -> x2, waiting for transfers between devices: 0.01 us -> 45.9 us  [the longest x1 27.6 us: local(): lax.psum((key_weight_grad, shared_grad), 'mp')]
    psum x1, blocking collectives: 38.6 us -> 10.1 us  [local(): lax.psum((key_weight_grad, shared_grad), 'mp')]
    unnamed x347 -> x349, local copies, waits for them, and re-layouts: 52.1 us -> 52.1 us
  transfers between devices with their start and end apart: 7 -> 8, of which waited for: 2 -> 5; matrix products, arithmetic and copies ran while one was open for 40% -> 38% of each run, Pallas kernels for 0% -> 0%
where the time goes in v1:
time: 1790 us; the launch traced here: 1770 us
  matrix products  457 us (26%)
  local copies, waits for them, and re-layouts  453 us (25%)
  other arithmetic  428 us (24%)
  waiting for transfers between devices  228 us (13%)
  blocking collectives  183 us (10%)
  between operations  18.5 us (1%)
    dot_general x6, matrix products, within_blocks(): jnp.einsum('bhij,bjhp->bihp', weights, values_blk, precision=PRECISE)  219 us
    psum x1, blocking collectives, local(): block_total, params_total = lax.psum((block_grad, params_grad), 'dp')  152 us
    dynamic_slice x192, local copies, waits for them, and re-layouts, state_mix(): lax.scan(carry_state, initial, (local_state, log_decay[:, :, -1], keep_fl...  105 us
    reduce_scatter x1, waiting for transfers between devices, local(): lax.psum_scatter(lax.dot_general(rows_in, w_in_flat, (((1,), (1,)), ((),...  96.8 us
    dynamic_update_slice x64, other arithmetic, state_mix(): lax.scan(carry_state, initial, (local_state, log_decay[:, :, -1], keep_fl...  65.5 us
    dot_general x6, matrix products, within_blocks(): jnp.einsum('bjn,bhj,bjhp->bhnp', b_blk, tail_decay, values_blk, precision...  61.1 us
    reduce_sum x32, other arithmetic, carry_state(): new_state = entering * jnp.exp(total_decay)[:, None, None] + local_state  54.8 us
    unnamed x349, local copies, waits for them, and re-layouts  52.1 us
  transfers between devices with their start and end apart: 8, of which 5 were waited for; matrix products, arithmetic and copies ran while one was open for 38% of the time, Pallas kernels for 0%

profile of v1, /device:TPU:0, one launch (start us, length us, event | category | flops | bytes accessed | tf_op | source)
XLA Modules:
  0.0 1770.0 jit_solution(13269272587551942200)
XLA Ops:
  21.4 45.3 %all-gather.9.cloned.1.call-done = bf16[8,1,768,194]{2,3,1,0:T(8,128)(2,1)} async-done(((bf16[1,1,768,194]{2,3,1,0:T(8,128)(2,1)}), bf16[8,1,768,194]{2,3,1,0:T(8,128)(2,1)}) %all-gather.9.cloned.1.call-update) | async-done | bytes 2383888 | tf_op jit(solution)/shard_map/all_gather | solution.py:160
  74.7 39.1 %all-gather.5.cloned.1.call-done = bf16[4096,768]{1,0:T(8,128)(2,1)} async-done(((bf16[1024,768]{1,0:T(8,128)(2,1)}), bf16[4096,768]{1,0:T(8,128)(2,1)}) %all-gather.5.cloned.1.call-update) | async-done | bytes 6291472 | tf_op jit(solution)/shard_map/all_gather | solution.py:171
  118.6 8.9 fusion.121
  132.0 13.7 rev.33
  145.7 7.9 fusion.88
  173.2 28.8 %fusion.98 = (f32[4096,384]{0,1:T(8,128)}, f32[4096,384]{0,1:T(8,128)}) fusion(f32[384]{0:T(512)S(1)} %mul.996, pred[4096]{0:T(1024)(128)(4,1)S(1)} %get-tuple-element.1094, f32[384]{0:T(512)S(1)} %mul.993, pred[4096]{0:T(1024)(128)(4,1)S(1)} %get-tuple-element.1095, f32[384]{0:T(512)S(1)} %mul.990, pred[4096]{0:T(1024)(128)(4,1)S(1)} %get-tuple-element.1096, ...), kind=kLoop, calls=%fused_computation.187 | loop fusion | flops 37748736 | bytes 18913792 | tf_op jit(solution)/shard_map/jvp(jit(silu))/mul | solution.py:97
  202.0 20.0 %rev.30 = f32[4096,6,64]{0,2,1:T(8,128)} reverse(f32[4096,6,64]{0,2,1:T(8,128)} %bitcast.605), dimensions={0} | reverse | bytes 12582912 | tf_op jit(solution)/shard_map/jvp()/rev | solution.py:113
  222.1 9.0 fusion.169
  233.1 60.8 %while.74 = (s32[]{:T(128)}, f32[6,64,64]{2,1,0:T(8,128)S(1)}, f32[16,6,64,64]{3,2,1,0:T(8,128)}, f32[16,6]{1,0:T(8,128)S(1)}, f32[16,6,1,1]{1,3,2,0:T(1,128)S(1...) while((s32[]{:T(128)}, f32[6,64,64]{2,1,0:T(8,128)S(1)}, ...), condition=%wide.region_8.9_spmd.clone, body=%wide.region_7.8_spmd.clone.sunk | while | flops 147459 | bytes 985312 | solution.py:79
  302.9 11.2 fusion.166
  316.1 60.6 %while.73 = (s32[]{:T(128)}, f32[6,64,64]{2,1,0:T(8,128)S(1)}, f32[16,6,64,64]{3,2,1,0:T(8,128)}, f32[16,6]{1,0:T(8,128)S(1)}, f32[16,6,1,1]{1,3,2,0:T(1,128)S(1...) while((s32[]{:T(128)}, f32[6,64,64]{2,1,0:T(8,128)S(1)}, ...), condition=%wide.region_4.5_spmd.clone, body=%wide.region_3.4_spmd.clone.sunk | while | flops 147459 | bytes 985312 | solution.py:79
  376.7 16.6 rev.32
  411.2 29.4 %fusion.84 = f32[16,6,8,8,256]{4,3,2,1,0:T(8,128)S(1)} fusion(f32[16,256,6,64]{1,3,2,0:T(8,128)S(1)} %bitcast.666, f32[16,256,6]{1,2,0:T(8,128)S(1)} %get-tuple-element.1066, f32[16,6,256]{2,1,0:T(8,128)S(1)} %copy.611, f32[16,256,256]{2,1,0:T(8,128)S(1)} %fusion.278, f32[16,6,256]{2,1,0:T(8,128)S(1)} %get-tuple-element.1065, ...), kind=kOutput, calls=%fused_computation.144 | convolution fusion | flops 4866441216 | bytes 23429120 | tf_op jit(solution)/shard_map/jvp(bhij,bjhp->bihp)/dot_general | solution.py:52
  445.7 20.0 %rev.34 = f32[4096,6,64]{0,2,1:T(8,128)} reverse(f32[4096,6,64]{0,2,1:T(8,128)} %pad_select_fusion), dimensions={0} | reverse | bytes 12582912 | tf_op jit(solution)/shard_map/jvp()/rev | solution.py:111
  469.4 8.0 fusion.276
  477.4 7.1 fusion.277
  484.5 34.6 %fusion.85 = f32[16,6,8,8,256]{4,3,2,1,0:T(8,128)} fusion(f32[16,256,6,64]{1,3,2,0:T(8,128)} %bitcast.668, f32[16,256,6]{1,2,0:T(8,128)S(1)} %get-tuple-element.1064, f32[16,6,256]{2,1,0:T(8,128)S(1)} %copy.593, f32[16,256,256]{2,1,0:T(8,128)} %fusion.276, f32[16,6,256]{2,1,0:T(8,128)S(1)} %get-tuple-element.1063, pred[256,256]{1,0:T(8,128)(4,1)S(1)} %copy-done.80, ...), kind=kOutput, calls=%fused_computation.146 | convolution fusion | flops 4866441216 | bytes 23429120 | tf_op jit(solution)/shard_map/jvp(bhij,bjhp->bihp)/dot_general | solution.py:52
  525.5 9.0 multiply_reduce_fusion.16
  534.6 10.2 psum.56
  552.6 10.1 psum.57
  562.7 17.4 multiply_reduce_fusion.14
  580.2 20.2 %rev.35 = f32[4096,6,64]{0,2,1:T(8,128)} reverse(f32[4096,6,64]{0,2,1:T(8,128)} %get-tuple-element.1009), dimensions={0} | reverse | bytes 12582912 | tf_op jit(solution)/shard_map/transpose(jvp())/rev | solution.py:111
  600.4 12.5 slice_select_fusion.1
  639.3 7.5 fusion.164
  648.9 77.2 %while.76 = (s32[]{:T(128)}, f32[6,64,64]{2,1,0:T(8,128)S(1)}, f32[16,6,64,64]{3,2,1,0:T(8,128)}, f32[16,6]{1,0:T(8,128)S(1)}, f32[16,6,64,64]{2,3,1,0:T(8,128)}...) while((s32[]{:T(128)}, f32[6,64,64]{2,1,0:T(8,128)S(1)}, ...), condition=%wide.region_28.29_spmd.clone, body=%wide.region_26.28_spmd.clone.sunk | while | flops 172036 | bytes 1081748 | solution.py:79
  726.8 8.4 copy.797
  736.6 8.3 copy.795
  745.0 7.6 fusion.165
  754.6 87.3 %while.75 = (s32[]{:T(128)}, f32[6,64,64]{2,1,0:T(8,128)S(1)}, f32[16,6,64,64]{3,2,1,0:T(8,128)}, f32[16,6]{1,0:T(8,128)S(1)}, f32[16,6,64,64]{2,3,1,0:T(8,128)}...) while((s32[]{:T(128)}, f32[6,64,64]{2,1,0:T(8,128)S(1)}, ...), condition=%wide.region_16.17_spmd.clone, body=%wide.region_14.16_spmd.clone.sunk | while | flops 172036 | bytes 1081748 | solution.py:79
  842.2 8.3 copy.796
  859.5 7.3 fusion.281
  866.8 12.0 multiply_reduce_fusion.5
  879.7 8.0 fusion.282
  887.7 11.6 multiply_reduce_fusion.4
  900.4 35.4 %fusion.79 = f32[16,6,256,256]{3,2,1,0:T(8,128)} fusion(f32[16,256,6,64]{1,0,3,2:T(8,128)} %bitcast.598, f32[16,256,6,64]{1,0,3,2:T(8,128)} %bitcast.655), kind=kOutput, calls=%fused_computation.138 | convolution fusion | flops 4831838208 | bytes 37748736 | tf_op jit(solution)/shard_map/transpose(jvp(jvp()))/checkpoint/bhij,bjhp->bihp/dot_general | solution.py:52
  935.9 66.3 %fusion.35 = (f32[16,6,256]{2,1,0:T(8,128)}, f32[16,6,256]{2,1,0:T(8,128)}, f32[16,6,256]{2,1,0:T(8,128)}, f32[16,256,256]{2,1,0:T(8,128)}, f32[16,256,256]{2,1,...) fusion(f32[16,6,256]{2,1,0:T(8,128)S(1)} %bitcast.704, ...), kind=kOutput, calls=%fused_computation.67 | convolution fusion | flops 5018337280 | bytes 55574528 | tf_op jit(solution)/shard_map/transpose(jvp(jvp()))/checkpoint/bhij,bjhp->bihp/dot_general | solution.py:52
  1003.4 9.1 fusion.185
  1012.5 27.1 %fusion.76 = f32[16,6,8,8,256]{4,3,2,1,0:T(8,128)} fusion(f32[16,256,6,64]{1,3,2,0:T(8,128)S(1)} %copy-done.38, f32[16,256,6]{1,2,0:T(8,128)S(1)} %get-tuple-element.1056, f32[16,6,256]{2,1,0:T(8,128)S(1)} %bitcast.703, f32[16,256,256]{2,1,0:T(8,128)} %fusion.282, f32[16,6,256]{2,1,0:T(8,128)S(1)} %copy-done.78, pred[256,256]{1,0:T(8,128)(4,1)S(1)} %copy-done.81, ...), kind=kOutput, calls=%fused_computation.134 | convolution fusion | flops 4866441216 | bytes 23429120 | tf_op jit(solution)/shard_map/transpose(jvp(jvp()))/checkpoint/bhij,bjhp->bihp/dot_general | solution.py:52
  1050.4 7.3 copy.791
  1060.3 8.3 fusion.180
  1068.7 26.4 %fusion.77 = f32[16,6,8,8,256]{4,3,2,1,0:T(8,128)} fusion(f32[16,256,6,64]{1,3,2,0:T(8,128)S(1)} %bitcast.682, f32[16,256,6]{1,2,0:T(8,128)S(1)} %get-tuple-element.1054, f32[16,6,256]{2,1,0:T(8,128)S(1)} %bitcast.705, f32[16,256,256]{2,1,0:T(8,128)S(1)} %copy-done.42, f32[16,6,256]{2,1,0:T(8,128)S(1)} %copy-done.77, pred[256,256]{1,0:T(8,128)(4,1)S(1)} %copy-done.81, ...), kind=kOutput, calls=%fused_computation.136 | convolution fusion | flops 4866441216 | bytes 23429120 | tf_op jit(solution)/shard_map/transpose(jvp(jvp()))/checkpoint/bhij,bjhp->bihp/dot_general | solution.py:52
  1110.5 20.0 %rev.37 = f32[4096,6,64]{0,2,1:T(8,128)} reverse(f32[4096,6,64]{0,2,1:T(8,128)} %bitcast.665), dimensions={0} | reverse | bytes 12582912 | tf_op jit(solution)/shard_map/transpose(jvp())/rev | solution.py:113
  1130.5 14.9 reduce-window.50
  1147.2 10.2 rev.39
  1162.6 10.2 rev.38
  1173.5 19.2 %multiply_reduce_fusion.23 = (f32[256]{0:T(256)}, f32[256]{0:T(256)}, f32[256]{0:T(256)}, f32[256]{0:T(256)}, f32[256]{0:T(256)}, /*index=5*/f32[256]{0:T(256)}, f32[256]{0:T(256)}, f32[4096,256]{1,0:T(8,128)S(1)}) fusion(f32[4096,256]{1,0:T(8,128)} %copy-done.13, pred[4096]{0:T(1024)(128)(4,1)S(1)} %copy-done.60, pred[4096]{0:T(1024)(128)(4,1)S(1)} %copy-done.66, ...), kind=kLoop, calls=%fused_computation.229 | loop fusion | flops 34601216 | bytes 16813056 | tf_op jit(solution)/shard_map/transpose(jvp())/reduce_sum | solution.py:34
  1206.4 14.9 reduce-window.56
  1228.7 12.0 add_add_fusion
  1240.8 16.0 multiply_reduce_fusion.13
  1256.9 16.7 multiply_select_fusion.8
  1273.6 21.3 %pad_add_fusion = f32[4096,384]{0,1:T(8,128)} fusion(f32[4096,384]{0,1:T(8,128)} %get-tuple-element.1032, f32[4096,384]{0,1:T(8,128)} %get-tuple-element.1033, f32[4096,384]{0,1:T(8,128)} %get-tuple-element.1034, f32[4096,384]{0,1:T(8,128)} %get-tuple-element.1035, f32[4096,384]{0,1:T(8,128)} %get-tuple-element.1036, f32[4096,384]{0,1:T(8,128)} %get-tuple-element.1037, ...), kind=kLoop, calls=%fused_computation.121 | loop fusion | flops 9437184 | bytes 50331648 | tf_op jit(solution)/shard_map/transpose(jvp())/add_any | solution.py:32
  1297.7 8.4 add_convert_fusion
  1306.1 27.6 %all-reduce.55.cloned.1.call-done = f32[768,256]{1,0:T(8,128)} async-done(((f32[768,256]{1,0:T(8,128)}), f32[768,256]{1,0:T(8,128)}) %all-reduce.55.cloned.1.call-update) | async-done | bytes 786448 | tf_op jit(solution)/shard_map/psum | solution.py:249
  1333.8 12.3 convolution_bitcast_fusion
  1346.8 11.0 convolution_bitcast_fusion.1
  1359.7 8.9 convert_element_type.65
  1368.8 9.0 dot_general.202
  1377.8 7.2 fusion.173
  1393.9 18.3 %all-reduce.57.cloned.1.call-done = f32[768,256]{1,0:T(8,128)} async-done(((f32[768,256]{1,0:T(8,128)}), f32[768,256]{1,0:T(8,128)}) %all-reduce.57.cloned.1.call-update) | async-done | bytes 786448 | tf_op jit(solution)/shard_map/psum | solution.py:249
  1416.2 96.8 %reduce-scatter.6.cloned.1.call-done = f32[1024,768]{1,0:T(8,128)} async-done(((f32[4096,768]{1,0:T(8,128)}), f32[1024,768]{1,0:T(8,128)}) %reduce-scatter.6.cloned.1.call-update) | async-done | bytes 3145744 | tf_op jit(solution)/shard_map/reduce_scatter | solution.py:230
  1517.8 10.1 psum.62
  1527.9 152.5 %all-reduce.58 = (bf16[6,768,194]{1,2,0:T(8,128)(2,1)S(1)}, f32[6,10,64]{2,0,1:T(8,128)S(1)}, f32[10,256]{1,0:T(8,128)S(1)}) all-reduce(f32[6,768,194]{1,2,0:T(8,128)} %pad_maximum_fusion, f32[6,10,64]{2,0,1:T(8,128)S(1)} %fusion.243, f32[10,256]{1,0:T(8,128)S(1)} %psum.62), channel_id=1, replica_groups=mesh['dp'=8,'mp'=4] {'dp'}, use_global_device_ids=true, to_apply=%region_44.45 | all-reduce | flops 900352 | bytes 5414912 | tf_op jit(solution)/shard_map/psum | solution.py:248
  1680.3 27.5 %fusion.117 = f32[1,768,194]{0,1,2:T(8,128)} fusion(bf16[6,768,194]{1,2,0:T(8,128)(2,1)S(1)} %get-tuple-element.986, s32[]{:T(128)S(6)} %axis_index.25, s32[24]{0:T(128)S(1)} %copy-done.136, s32[]{:T(128)S(6)} %select_n.236), kind=kOutput, calls=%fused_computation.213 | convolution fusion | flops 1787910 | bytes 2383976 | tf_op jit(solution)/shard_map/dot_general | solution.py:256
  1707.9 40.9 %copy.735 = f32[1,768,194]{1,2,0:T(8,128)} copy(f32[1,768,194]{0,1,2:T(8,128)} %fusion.117) | data formatting | bytes 1191936 | tf_op jit(solution)/shard_map/dot_general | solution.py:256
  (1052 shorter events, 525.1 us)
Async XLA Ops:
  7.2 59.5 %all-gather.9.cloned.1.call-start = ((), (), s32[]{:S(2)}) async-start(), calls=%async_computation.10 | async-start | bytes 2764800 | tf_op jit(solution)/shard_map/all_gather | solution.py:160
  9.1 104.7 %all-gather.5.cloned.1.call-start = ((), (), s32[]{:S(2)}) async-start(), calls=%async_computation.3 | async-start | bytes 7864320 | tf_op jit(solution)/shard_map/all_gather | solution.py:171
  9.9 56.9 %copy-start.84 = (f32[768]{0:T(1024)}, f32[768]{0:T(1024)S(1)}, u32[]{:S(2)}) copy-start(f32[768]{0:T(1024)S(1)} %mul.974) | copy-start | bytes 9220
  15.9 528.9 %all-gather.7.cloned.1.call-start = ((), (), s32[]{:S(2)}) async-start(), calls=%async_computation.5 | async-start | bytes 7864320 | tf_op jit(solution)/shard_map/all_gather | solution.py:198
  16.6 1278.3 %reduce-scatter.8.cloned.1.call-start = ((), (), s32[]{:S(2)}) async-start(), calls=%async_computation.7 | async-start | bytes 5242880 | tf_op jit(solution)/shard_map/reduce_scatter | solution.py:216
  17.6 100.9 %copy-start.119 = (f32[1,256]{1,0:T(1,128)}, f32[1,256]{1,0:T(1,128)S(1)}, u32[]{:S(2)}) copy-start(f32[1,256]{1,0:T(1,128)S(1)} %get-tuple-element.1078) | copy-start | bytes 3076
  17.6 100.9 %copy-start.121 = (f32[1,256]{1,0:T(1,128)}, f32[1,256]{1,0:T(1,128)S(1)}, u32[]{:S(2)}) copy-start(f32[1,256]{1,0:T(1,128)S(1)} %get-tuple-element.1079) | copy-start | bytes 3076
  17.6 100.9 %copy-start.123 = (f32[1,256]{1,0:T(1,128)}, f32[1,256]{1,0:T(1,128)S(1)}, u32[]{:S(2)}) copy-start(f32[1,256]{1,0:T(1,128)S(1)} %get-tuple-element.1080) | copy-start | bytes 3076
  17.7 100.9 %copy-start.125 = (f32[1,256]{1,0:T(1,128)}, f32[1,256]{1,0:T(1,128)S(1)}, u32[]{:S(2)}) copy-start(f32[1,256]{1,0:T(1,128)S(1)} %get-tuple-element.1081) | copy-start | bytes 3076
  17.7 100.9 %copy-start.127 = (f32[1,256]{1,0:T(1,128)}, f32[1,256]{1,0:T(1,128)S(1)}, u32[]{:S(2)}) copy-start(f32[1,256]{1,0:T(1,128)S(1)} %get-tuple-element.1082) | copy-start | bytes 3076
  17.7 100.9 %copy-start.129 = (f32[1,256]{1,0:T(1,128)}, f32[1,256]{1,0:T(1,128)S(1)}, u32[]{:S(2)}) copy-start(f32[1,256]{1,0:T(1,128)S(1)} %get-tuple-element.1083) | copy-start | bytes 3076
  17.7 100.9 %copy-start.131 = (f32[1,256]{1,0:T(1,128)}, f32[1,256]{1,0:T(1,128)S(1)}, u32[]{:S(2)}) copy-start(f32[1,256]{1,0:T(1,128)S(1)} %get-tuple-element.1084) | copy-start | bytes 3076
  17.7 139.2 %copy-start.90 = (f32[6,2]{1,0:T(8,128)}, f32[6,2]{1,0:T(8,128)S(1)}, u32[]{:S(2)}) copy-start(f32[6,2]{1,0:T(8,128)S(1)} %slice_bitcast_fusion.4) | copy-start | bytes 148
  17.7 507.8 %copy-start.94 = (f32[6,64]{1,0:T(8,128)}, f32[6,64]{1,0:T(8,128)S(1)}, u32[]{:S(2)}) copy-start(f32[6,64]{1,0:T(8,128)S(1)} %get-tuple-element.1068) | copy-start | bytes 4612
  17.7 545.0 %copy-start.92 = (f32[6,64]{1,0:T(8,128)}, f32[6,64]{1,0:T(8,128)S(1)}, u32[]{:S(2)}) copy-start(f32[6,64]{1,0:T(8,128)S(1)} %get-tuple-element.1067) | copy-start | bytes 4612
  19.5 153.6 %copy-start.55 = (pred[4096]{0:T(1024)(128)(4,1)}, pred[4096]{0:T(1024)(128)(4,1)S(1)}, u32[]{:S(2)}) copy-start(pred[4096]{0:T(1024)(128)(4,1)S(1)} %get-tuple-element.1096) | copy-start | bytes 12292
  19.5 153.6 %copy-start.57 = (pred[4096]{0:T(1024)(128)(4,1)}, pred[4096]{0:T(1024)(128)(4,1)S(1)}, u32[]{:S(2)}) copy-start(pred[4096]{0:T(1024)(128)(4,1)S(1)} %get-tuple-element.1097) | copy-start | bytes 12292
  19.7 153.4 %copy-start.59 = (pred[4096]{0:T(1024)(128)(4,1)}, pred[4096]{0:T(1024)(128)(4,1)S(1)}, u32[]{:S(2)}) copy-start(pred[4096]{0:T(1024)(128)(4,1)S(1)} %get-tuple-element.1094) | copy-start | bytes 12292
  19.8 153.4 %copy-start.61 = (pred[4096]{0:T(1024)(128)(4,1)}, pred[4096]{0:T(1024)(128)(4,1)S(1)}, u32[]{:S(2)}) copy-start(pred[4096]{0:T(1024)(128)(4,1)S(1)} %get-tuple-element.1095) | copy-start | bytes 12292
  20.0 153.1 %copy-start.63 = (pred[4096]{0:T(1024)(128)(4,1)}, pred[4096]{0:T(1024)(128)(4,1)S(1)}, u32[]{:S(2)}) copy-start(pred[4096]{0:T(1024)(128)(4,1)S(1)} %get-tuple-element.1098) | copy-start | bytes 12292
  20.0 153.1 %copy-start.65 = (pred[4096]{0:T(1024)(128)(4,1)}, pred[4096]{0:T(1024)(128)(4,1)S(1)}, u32[]{:S(2)}) copy-start(pred[4096]{0:T(1024)(128)(4,1)S(1)} %get-tuple-element.1099) | copy-start | bytes 12292
  20.2 152.9 %copy-start.67 = (pred[4096]{0:T(1024)(128)(4,1)}, pred[4096]{0:T(1024)(128)(4,1)S(1)}, u32[]{:S(2)}) copy-start(pred[4096]{0:T(1024)(128)(4,1)S(1)} %get-tuple-element.1101) | copy-start | bytes 12292
  21.0 152.2 %copy-start.97 = (f32[384]{0:T(512)}, f32[384]{0:T(512)S(1)}, u32[]{:S(2)}) copy-start(f32[384]{0:T(512)S(1)} %mul.978) | copy-start | bytes 4612
  21.0 152.1 %copy-start.99 = (f32[384]{0:T(512)}, f32[384]{0:T(512)S(1)}, u32[]{:S(2)}) copy-start(f32[384]{0:T(512)S(1)} %mul.996) | copy-start | bytes 4612
  21.1 152.1 %copy-start.101 = (f32[384]{0:T(512)}, f32[384]{0:T(512)S(1)}, u32[]{:S(2)}) copy-start(f32[384]{0:T(512)S(1)} %mul.993) | copy-start | bytes 4612
  21.2 152.0 %copy-start.103 = (f32[384]{0:T(512)}, f32[384]{0:T(512)S(1)}, u32[]{:S(2)}) copy-start(f32[384]{0:T(512)S(1)} %mul.990) | copy-start | bytes 4612
  21.3 151.9 %copy-start.105 = (f32[384]{0:T(512)}, f32[384]{0:T(512)S(1)}, u32[]{:S(2)}) copy-start(f32[384]{0:T(512)S(1)} %mul.987) | copy-start | bytes 4612
  21.3 151.9 %copy-start.107 = (f32[384]{0:T(512)}, f32[384]{0:T(512)S(1)}, u32[]{:S(2)}) copy-start(f32[384]{0:T(512)S(1)} %mul.984) | copy-start | bytes 4612
  21.4 151.8 %copy-start.109 = (f32[384]{0:T(512)}, f32[384]{0:T(512)S(1)}, u32[]{:S(2)}) copy-start(f32[384]{0:T(512)S(1)} %mul.981) | copy-start | bytes 4612
  69.1 44.7 %copy-start.35 = (f32[768,256]{1,0:T(8,128)S(1)}, f32[768,256]{1,0:T(8,128)}, u32[]{:S(2)}) copy-start(f32[768,256]{1,0:T(8,128)} %param.42) | copy-start | bytes 2359300
  376.7 26.1 %copy-start.134 = (f32[16,6,1,1]{1,3,2,0:T(1,128)}, f32[16,6,1,1]{1,3,2,0:T(1,128)S(1)}, u32[]{:S(2)}) copy-start(f32[16,6,1,1]{1,3,2,0:T(1,128)S(1)} %get-tuple-element.1391) | copy-start | bytes 1156
  477.4 48.1 %slice-start.4 = ((s8[6291456]{0:T(1024)(128)(4,1)}), s8[4194304]{0:T(1024)(128)(4,1)S(1)}, s32[]{:S(2)}) async-start(s8[6291456]{0:T(1024)(128)(4,1)} %bitcast.608), calls=%async_computation.15 | async-start | bytes 8388608
  477.4 48.1 %slice-start.14 = ((s8[6291456]{0:T(1024)(128)(4,1)}), s8[4194304]{0:T(1024)(128)(4,1)S(1)}, s32[]{:S(2)}) async-start(s8[6291456]{0:T(1024)(128)(4,1)} %bitcast.659), calls=%async_computation.25 | async-start | bytes 8388608
  484.5 41.0 %slice-start.5 = ((s8[6291456]{0:T(1024)(128)(4,1)}), s8[2097152]{0:T(1024)(128)(4,1)S(1)}, s32[]{:S(2)}) async-start(s8[6291456]{0:T(1024)(128)(4,1)} %bitcast.608), calls=%async_computation.16 | async-start | bytes 4194304
  484.5 41.0 %slice-start.15 = ((s8[6291456]{0:T(1024)(128)(4,1)}), s8[2097152]{0:T(1024)(128)(4,1)S(1)}, s32[]{:S(2)}) async-start(s8[6291456]{0:T(1024)(128)(4,1)} %bitcast.659), calls=%async_computation.26 | async-start | bytes 4194304
  580.2 20.2 %copy-start.117 = (pred[4095]{0:T(1024)(128)(4,1)S(1)}, pred[4095]{0:T(1024)(128)(4,1)}, u32[]{:S(2)}) copy-start(pred[4095]{0:T(1024)(128)(4,1)} %slice.312) | copy-start | bytes 12289
  859.2 198.5 %copy-start.47 = (f32[16,6,256]{2,0,1:T(8,128)}, f32[16,6,256]{2,0,1:T(8,128)S(1)}, u32[]{:S(2)}) copy-start(f32[16,6,256]{2,0,1:T(8,128)S(1)} %copy_bitcast_fusion.5) | copy-start | bytes 294916
  900.4 35.4 %copy-start.74 = (f32[16,256,6]{1,2,0:T(8,128)S(1)}, f32[16,256,6]{1,2,0:T(8,128)}, u32[]{:S(2)}) copy-start(f32[16,256,6]{1,2,0:T(8,128)} %copy.964) | copy-start | bytes 294916
  900.4 35.4 %copy-start.75 = (f32[16,256,6]{1,2,0:T(8,128)S(1)}, f32[16,256,6]{1,2,0:T(8,128)}, u32[]{:S(2)}) copy-start(f32[16,256,6]{1,2,0:T(8,128)} %copy.965) | copy-start | bytes 294916
  900.4 35.4 %copy-start.81 = (pred[256,256]{1,0:T(8,128)(4,1)S(1)}, pred[256,256]{1,0:T(8,128)(4,1)}, u32[]{:S(2)}) copy-start(pred[256,256]{1,0:T(8,128)(4,1)} %iota_compare_fusion) | copy-start | bytes 196612
  935.8 67.5 %slice-start.2 = ((s8[6291456]{0:T(1024)(128)(4,1)}), s8[4194304]{0:T(1024)(128)(4,1)S(1)}, s32[]{:S(2)}) async-start(s8[6291456]{0:T(1024)(128)(4,1)} %bitcast.602), calls=%async_computation.13 | async-start | bytes 8388608
  935.8 66.3 %copy-start.53 = (f32[16,6,256]{2,1,0:T(8,128)S(1)}, f32[16,6,256]{2,1,0:T(8,128)}, u32[]{:S(2)}) copy-start(f32[16,6,256]{2,1,0:T(8,128)} %fusion.207) | copy-start | bytes 294916
  935.8 67.5 %slice-start.3 = ((s8[6291456]{0:T(1024)(128)(4,1)}), s8[2097152]{0:T(1024)(128)(4,1)S(1)}, s32[]{:S(2)}) async-start(s8[6291456]{0:T(1024)(128)(4,1)} %bitcast.602), calls=%async_computation.14 | async-start | bytes 4194304
  935.8 67.5 %copy-start.15 = (f32[16,6,64,64]{3,2,1,0:T(8,128)S(1)}, f32[16,6,64,64]{3,2,1,0:T(8,128)}, u32[]{:S(2)}) copy-start(f32[16,6,64,64]{3,2,1,0:T(8,128)} %get-tuple-element.512) | copy-start | bytes 4718596
  1012.5 27.2 %copy-start.8 = (f32[4096,64]{1,0:T(8,128)S(1)}, f32[4096,64]{1,0:T(8,128)}, u32[]{:S(2)}) copy-start(f32[4096,64]{1,0:T(8,128)} %get-tuple-element.1045) | copy-start | bytes 3145732
  1012.5 27.2 %copy-start.30 = (f32[16,256,256]{2,1,0:T(8,128)S(1)}, f32[16,256,256]{2,1,0:T(8,128)}, u32[]{:S(2)}) copy-start(f32[16,256,256]{2,1,0:T(8,128)} %get-tuple-element.914) | copy-start | bytes 12582916
  1012.5 27.2 %copy-start.45 = (f32[16,256,64]{1,2,0:T(8,128)S(1)}, f32[16,256,64]{1,2,0:T(8,128)}, u32[]{:S(2)}) copy-start(f32[16,256,64]{1,2,0:T(8,128)} %fusion.178) | copy-start | bytes 3145732
  1068.7 26.4 %copy-start.29 = (f32[16,256,256]{2,1,0:T(8,128)S(1)}, f32[16,256,256]{2,1,0:T(8,128)}, u32[]{:S(2)}) copy-start(f32[16,256,256]{2,1,0:T(8,128)} %get-tuple-element.895) | copy-start | bytes 12582916
  1068.7 26.4 %copy-start.44 = (f32[16,256,64]{1,2,0:T(8,128)S(1)}, f32[16,256,64]{1,2,0:T(8,128)}, u32[]{:S(2)}) copy-start(f32[16,256,64]{1,2,0:T(8,128)} %fusion.179) | copy-start | bytes 3145732
  1173.4 19.3 %copy-start.120 = (f32[1,256]{1,0:T(1,128)S(1)}, f32[1,256]{1,0:T(1,128)}, u32[]{:S(2)}) copy-start(f32[1,256]{1,0:T(1,128)} %copy-done.119) | copy-start | bytes 3076
  1173.4 19.3 %copy-start.122 = (f32[1,256]{1,0:T(1,128)S(1)}, f32[1,256]{1,0:T(1,128)}, u32[]{:S(2)}) copy-start(f32[1,256]{1,0:T(1,128)} %copy-done.121) | copy-start | bytes 3076
  1206.1 20.5 %copy-start.91 = (f32[6,2]{1,0:T(8,128)S(1)}, f32[6,2]{1,0:T(8,128)}, u32[]{:S(2)}) copy-start(f32[6,2]{1,0:T(8,128)} %copy-done.90) | copy-start | bytes 148
  1206.1 22.6 %copy-start.95 = (f32[6,64]{1,0:T(8,128)S(1)}, f32[6,64]{1,0:T(8,128)}, u32[]{:S(2)}) copy-start(f32[6,64]{1,0:T(8,128)} %copy-done.94) | copy-start | bytes 4612
  1206.1 127.6 %all-reduce.55.cloned.1.call-start = ((), (), s32[]{:S(2)}) async-start(), calls=%async_computation.8 | async-start | bytes 1572864 | tf_op jit(solution)/shard_map/psum | solution.py:249
  1273.6 21.3 %copy-start.39 = (bf16[1024,768]{1,0:T(8,128)(2,1)S(1)}, bf16[1024,768]{1,0:T(8,128)(2,1)}, u32[]{:S(2)}) copy-start(bf16[1024,768]{1,0:T(8,128)(2,1)} %fusion.124) | copy-start | bytes 4718596
  1297.6 114.6 %all-reduce.57.cloned.1.call-start = ((), (), s32[]{:S(2)}) async-start(), calls=%async_computation.9 | async-start | bytes 1572864 | tf_op jit(solution)/shard_map/psum | solution.py:249
  1297.7 36.1 %copy-start.34 = (bf16[6,768,194]{1,2,0:T(8,128)(2,1)S(1)}, bf16[6,768,194]{1,2,0:T(8,128)(2,1)}, u32[]{:S(2)}) copy-start(bf16[6,768,194]{1,2,0:T(8,128)(2,1)} %copy-done.33) | copy-start | bytes 5363716
  1333.7 179.3 %reduce-scatter.6.cloned.1.call-start = ((), (), s32[]{:S(2)}) async-start(), calls=%async_computation.6 | async-start | bytes 15728640 | tf_op jit(solution)/shard_map/reduce_scatter | solution.py:230
  1346.1 411.6 %reduce-scatter.4.cloned.1.call-start = ((), (), s32[]{:S(2)}) async-start(), calls=%async_computation.4 | async-start | bytes 15728640 | tf_op jit(solution)/shard_map/reduce_scatter | solution.py:191
  1391.6 20.6 %copy-start.36 = (f32[768,256]{1,0:T(8,128)S(1)}, f32[768,256]{1,0:T(8,128)}, u32[]{:S(2)}) copy-start(f32[768,256]{1,0:T(8,128)} %param.42) | copy-start | bytes 2359300
  1391.6 121.5 %copy-start.25 = (bf16[1024,768]{1,0:T(8,128)(2,1)S(1)}, bf16[1024,768]{1,0:T(8,128)(2,1)}, u32[]{:S(2)}) copy-start(bf16[1024,768]{1,0:T(8,128)(2,1)} %param.30) | copy-start | bytes 4718596
  1391.6 121.4 %copy-start.49 = (f32[1024,256]{1,0:T(8,128)S(1)}, f32[1024,256]{1,0:T(8,128)}, u32[]{:S(2)}) copy-start(f32[1024,256]{1,0:T(8,128)} %reduce-scatter.8.cloned.1.call-done) | copy-start | bytes 3145732
  1391.6 121.4 %copy-start.83 = (f32[1024]{0:T(1024)S(1)}, f32[1024]{0:T(1024)}, u32[]{:S(2)}) copy-start(f32[1024]{0:T(1024)} %copy-done.82) | copy-start | bytes 12292
  1391.6 121.4 %copy-start.85 = (f32[768]{0:T(1024)S(1)}, f32[768]{0:T(1024)}, u32[]{:S(2)}) copy-start(f32[768]{0:T(1024)} %copy-done.84) | copy-start | bytes 9220
  (115 other events, 1035.2 us)
Sparse Core Ops, SparseCore 0:
  10.8 55.9 all-gather.8
  68.9 44.9 all-gather.4
  115.4 46.3 all-gather.6
  1206.2 45.8 reduce-scatter.7
  1297.7 35.9 all-reduce.54
  1337.4 74.8 all-reduce.56
  1414.8 98.1 reduce-scatter.5
  1515.6 99.0 reduce-scatter.3
